TPU v7x, 512 devices: a whole 4x8x8 slice. The times are simulated.
512 devices in a mesh: pulse: 8 (over x, core), range: 64 (over z, y).
Axes of the slice: x: 4, y: 8, z: 8, core: 2. Of those that a mesh axis runs over, the one named last changes fastest.
Arguments:
- echoes: bfloat16 [2, 2048, 32768], P(None, ('pulse', 'range')), may hold values from -6 to 6
- range_filter: float32 [2, 32768], replicated, may hold values from -6 to 6
- shift_table: int32 [32768], replicated, may hold values from -12 to 12
- tap_table: int32 [32768], replicated, may hold values from 0 to 15
- kernels: float32 [16, 8], replicated, may hold values from -2 to 2
- tail_lengths: int32 [256], P('range'), may hold values from 32 to 128, as said below
- azimuth_rate: float32 [32768], P('range'), may hold values from 0.5 to 4
Outputs:
- focused: bfloat16 [2, 2048, 32768], P(None, 'pulse', 'range')
Inputs may be any that keep to these rules, and one draw needn't show every extreme that they name: `tail_lengths`: some range block has a tail of exactly 128 pulses and some of exactly 32.
All inputs are finite; a program needn't handle non-finite values.
Results may differ from a plain program's by a relative error of at most 0.0099.
Values may be sent and summed in bfloat16 or wider, within the bound.
A program may use at most 64 MiB of HBM per device.

v0:
```python
import math

import jax
import jax.numpy as jnp
import numpy as np
from jax import lax
from jax.experimental import pallas as pl
from jax.experimental.pallas import tpu as pltpu
from jax.sharding import PartitionSpec as P

RA = 256
RB = 128
TMAX = 128
NK = 16
RBLK = 128
NR = 64
PD = 4
MSG = 40
F32 = jnp.float32
BF16 = jnp.bfloat16
MESH = pl.DeviceIdType.MESH


def table(rows, cols, length):
    prod = (np.asarray(rows)[:, None] * np.asarray(cols)[None, :]) % length
    angle = prod.astype(np.float32) * np.float32(-2.0 * math.pi / length)
    return np.cos(angle).astype(np.float32), np.sin(angle).astype(np.float32)


def bf(value):
    return np.asarray(value).astype(jnp.bfloat16)


def range_constants():
    ra = np.arange(RA)
    wr, wi = table(ra, ra, RA)
    first = bf(np.block([[wr, -wi], [wi, wr]]))
    vr, vi = table(np.arange(RB), np.arange(RB), RB)
    second = bf(np.block([[vr, vi], [-vi, vr]]))
    third = bf(np.block([[vr, -vi], [vi, vr]]))
    real = np.concatenate([wr, wi], 1)
    imag = np.concatenate([-wi, wr], 1)
    both = np.stack([real, imag])
    main = both.reshape(2, NR, 4, 2 * RA).transpose(1, 0, 2, 3).reshape(8 * NR, 2 * RA)
    zero = np.zeros((2, 1, 2 * RA), np.float32)
    right = np.concatenate([both[:, 4::4], zero], 1).reshape(2 * NR, 2 * RA)
    left = np.concatenate([zero, both[:, 3:-1:4]], 1).reshape(2 * NR, 2 * RA)
    inverse = bf(bf(np.concatenate([main, right, left], 0)).astype(np.float32) * np.float32(2.0**-15))
    tr, ti = table(ra, np.arange(RB), RA * RB)
    return first, second, third, inverse, np.stack([tr, ti])


def azimuth_constants():
    seq = 384
    half = seq // 2
    freq = np.concatenate([np.arange(half), [half], seq - np.arange(1, half)])
    tail = np.array([4 * s + p for p in range(PD) for s in range(NR // 2)])
    own = np.array([TMAX + 4 * s + p for p in range(PD) for s in range(NR)])
    rows = np.concatenate([own, tail])
    wr, wi = table(freq, rows, seq)
    no = own.size
    fr = [wr[:, :no], -wi[:, :no], wr[:, no:], -wi[:, no:]]
    fi = [wi[:, :no], wr[:, :no], wi[:, no:], wr[:, no:]]
    forward = bf(np.concatenate([np.concatenate(fr, 1), np.concatenate(fi, 1)], 0))
    out_rows = TMAX + np.arange(seq - TMAX)
    ur, ui = table(out_rows, freq, seq)
    inverse = bf(np.block([[ur, ui], [-ui, ur]]))
    return forward, inverse


def dot(a, b):
    return jnp.dot(a, b, preferred_element_type=F32)


def compress_kernel(x_ref, rf_ref, w1_ref, v2_ref, v3_ref, w6_ref, tw_ref, out_ref, xs, xb, gb, hs, es):
    for c in range(2):
        xs[c] = x_ref[c].astype(F32)
    for c in range(2):
        for p in range(PD):
            xb[c * RA : (c + 1) * RA, p * RB : (p + 1) * RB] = xs[c, pl.ds(p, RA, stride=PD), :].astype(BF16)
    for c in range(2):
        for h in range(2):
            part = rf_ref[pl.ds(2 * h + c, RB, stride=4), :]
            hs[c, h * RB : (h + 1) * RB, :] = part.T
    twr, twi = tw_ref[0], tw_ref[1]
    for u in range(2):
        s1 = dot(w1_ref[...], xb[:, 256 * u : 256 * (u + 1)])
        for v in range(2):
            p = 2 * u + v
            re = s1[:RA, v * RB : (v + 1) * RB]
            im = s1[RA:, v * RB : (v + 1) * RB]
            a = jnp.concatenate([re * twr - im * twi, re * twi + im * twr], axis=1).astype(BF16)
            t = dot(a, v2_ref[...])
            re, im = t[:, :RB], t[:, RB:]
            hr, hi = hs[0], hs[1]
            a = jnp.concatenate([re * hr - im * hi, re * hi + im * hr], axis=1).astype(BF16)
            t = dot(a, v3_ref[...])
            re, im = t[:, :RB], t[:, RB:]
            gb[:RA, p * RB : (p + 1) * RB] = (re * twr + im * twi).astype(BF16)
            gb[RA:, p * RB : (p + 1) * RB] = (im * twr - re * twi).astype(BF16)
    lane = lax.broadcasted_iota(jnp.int32, (2 * NR, RB), 1)
    for u in range(2):
        g = gb[:, 256 * u : 256 * (u + 1)]
        m = dot(w6_ref[: 8 * NR, :], g)
        e = dot(w6_ref[8 * NR :, :], g)
        parts = []
        for v in range(2):
            p = 2 * u + v
            parts.append(m[:, v * RB : (v + 1) * RB].reshape(NR, 8, RB))
            ev = e[:, v * RB : (v + 1) * RB]
            sel = jnp.where(lane < 64, ev[: 2 * NR], ev[2 * NR :])
            for c in range(2):
                es[pl.ds(2 * p + c, NR, stride=8), :] = sel[c * NR : (c + 1) * NR]
        out_ref[:, 16 * u : 16 * (u + 1), :] = jnp.concatenate(parts, axis=1).astype(BF16)
    out_ref[:, 32:40, :] = es[...].reshape(NR, 8, RB).astype(BF16)


def exchange_kernel(src_ref, dst_ref, send_sem, recv_sem, own_sem):
    me = lax.axis_index("range")
    barrier = pltpu.get_barrier_semaphore()

    def greet(i, carry):
        pl.semaphore_signal(barrier, inc=1, device_id={"range": lax.rem(me + i, NR)}, device_id_type=MESH)
        return carry

    lax.fori_loop(1, NR, greet, 0)
    own = pltpu.make_async_copy(src_ref.at[me], dst_ref.at[me], own_sem)
    own.start()
    pl.semaphore_wait(barrier, NR - 1)

    def copy(i):
        peer = lax.rem(me + i, NR)
        return pltpu.make_async_remote_copy(
            src_ref=src_ref.at[peer],
            dst_ref=dst_ref.at[me],
            send_sem=send_sem.at[i],
            recv_sem=recv_sem.at[i],
            device_id={"range": peer},
            device_id_type=MESH,
        )

    def send(i, carry):
        copy(i).start()
        return carry

    def finish(i, carry):
        copy(i).wait()
        return carry

    lax.fori_loop(1, NR, send, 0)
    own.wait()
    lax.fori_loop(1, NR, finish, 0)


def migrate_kernel(x_ref, shift_ref, tap_ref, kern_ref, out_ref, tail_ref, xs, yb, bm):
    xs[...] = x_ref[...].reshape(NR * MSG, RB).astype(F32)
    for c in range(2):
        for p in range(PD):
            rows = slice(c * 256 + p * NR, c * 256 + (p + 1) * NR)
            halo = xs[pl.ds(32 + 2 * p + c, NR, stride=MSG), :].astype(BF16)
            yb[rows, 0:RB] = halo
            yb[rows, 5 * RB : 6 * RB] = halo
            for j in range(4):
                block = xs[pl.ds(8 * p + 4 * c + j, NR, stride=MSG), :].astype(BF16)
                yb[rows, (j + 1) * RB : (j + 2) * RB] = block
    bm[...] = jnp.zeros_like(bm)
    taps = tap_ref[...]
    coef = jnp.zeros((8, 4 * RB), F32)
    for k in range(NK):
        coef = coef + jnp.where(taps == k, kern_ref[:, k : k + 1], 0.0)
    shifts = shift_ref[...]
    for j in range(4):
        row = lax.broadcasted_iota(jnp.int32, (160, RB), 0)
        col = lax.broadcasted_iota(jnp.int32, (160, RB), 1)
        lanes = slice(j * RB, (j + 1) * RB)
        tap = row - col - shifts[:, lanes] - 13
        part = jnp.zeros((160, RB), F32)
        for t in range(8):
            part = part + jnp.where(tap == t, coef[t : t + 1, lanes], 0.0)
        top = RB * (1 + j % 2) - 16
        bm[j // 2, top : top + 160, (j % 2) * RB : (j % 2 + 1) * RB] = part.astype(BF16)
    for u in range(2):
        got = dot(yb[:, 256 * u : 256 * u + 512], bm[u]).astype(BF16)
        cols = slice(256 * u, 256 * (u + 1))
        out_ref[:, cols] = got
        for c in range(2):
            for p in range(PD):
                tail_ref[c * 128 + p * 32 : c * 128 + (p + 1) * 32, cols] = got[
                    c * 256 + p * NR + 32 : c * 256 + (p + 1) * NR
                ]


def sincos(phase):
    turns = phase * (2.0 / math.pi)
    near = jnp.floor(turns + 0.5)
    z = (turns - near) * (math.pi / 2)
    z2 = z * z
    sin = z * (1.0 + z2 * (-1.0 / 6 + z2 * (1.0 / 120 + z2 * (-1.0 / 5040 + z2 * (1.0 / 362880)))))
    cos = 1.0 + z2 * (-0.5 + z2 * (1.0 / 24 + z2 * (-1.0 / 720 + z2 * (1.0 / 40320))))
    quad = near.astype(jnp.int32)
    odd = (quad & 1) == 1
    s = jnp.where(odd, cos, sin)
    c = jnp.where(odd, sin, cos)
    s = jnp.where((quad & 2) == 2, -s, s)
    c = jnp.where(((quad + 1) & 2) == 2, -c, c)
    return s, c


def azimuth_kernel(own_ref, tail_ref, len_ref, rate_ref, w_ref, u_ref, out_ref, zt, db):
    first = lax.axis_index("pulse") == 0
    row = lax.broadcasted_iota(jnp.int32, (TMAX, 256), 0)
    when = 4 * lax.rem(row, 32) + row // 32
    for u in range(2):
        cols = slice(256 * u, 256 * (u + 1))
        limit = jnp.where(first, 2 * TMAX, TMAX - len_ref[:, cols])
        inside = when >= limit
        for c in range(2):
            part = tail_ref[c * TMAX : (c + 1) * TMAX, cols].astype(F32)
            zt[c * TMAX : (c + 1) * TMAX, :] = jnp.where(inside, part, 0.0).astype(BF16)
        d = dot(w_ref[:, :512], own_ref[:, cols]) + dot(w_ref[:, 512:], zt[...])
        rate = rate_ref[:, cols]
        centre = lax.broadcasted_iota(jnp.int32, (192, 256), 0).astype(F32)
        s1, c1 = sincos(rate * (centre * centre) * (1.0 / 384))
        edge = lax.broadcasted_iota(jnp.int32, (8, 256), 0).astype(F32)
        edge = jnp.where(edge == 0.0, 192.0, edge)
        s2, c2 = sincos(rate * (edge * edge) * (1.0 / 384))
        for h in range(2):
            s = s1 if h == 0 else jnp.concatenate([s2, s1[8:]], axis=0)
            co = c1 if h == 0 else jnp.concatenate([c2, c1[8:]], axis=0)
            re = d[192 * h : 192 * (h + 1)]
            im = d[384 + 192 * h : 384 + 192 * (h + 1)]
            db[192 * h : 192 * (h + 1), :] = (re * co - im * s).astype(BF16)
            db[384 + 192 * h : 384 + 192 * (h + 1), :] = (re * s + im * co).astype(BF16)
        out = dot(u_ref[...], db[...]) * (1.0 / 384)
        out_ref[0, :, cols] = out[:256].astype(BF16)
        out_ref[1, :, cols] = out[256:].astype(BF16)


def vmem(count):
    return [pl.BlockSpec(memory_space=pltpu.VMEM)] * count


def per_device(echoes, range_filter, shift_table, tap_table, kernels, tail_lengths, azimuth_rate):
    bins = azimuth_rate.shape[0]
    x = echoes.reshape(2, PD, RA, RB).transpose(0, 2, 1, 3).reshape(2, RA * PD, RB)
    rf = range_filter.reshape(2, RA, RB).transpose(1, 0, 2).reshape(2 * RA, RB)
    w1, v2, v3, w6, tw = range_constants()
    sent = pl.pallas_call(
        compress_kernel,
        out_shape=jax.ShapeDtypeStruct((NR, MSG, RB), BF16),
        in_specs=vmem(7),
        out_specs=pl.BlockSpec(memory_space=pltpu.VMEM),
        scratch_shapes=[
            pltpu.VMEM((2, RA * PD, RB), F32),
            pltpu.VMEM((2 * RA, PD * RB), BF16),
            pltpu.VMEM((2 * RA, PD * RB), BF16),
            pltpu.VMEM((2, RA, RB), F32),
            pltpu.VMEM((8 * NR, RB), F32),
        ],
        name="compress",
    )(x, rf, w1, v2, v3, w6, tw)
    got = pl.pallas_call(
        exchange_kernel,
        out_shape=jax.ShapeDtypeStruct((NR, MSG, RB), BF16),
        in_specs=vmem(1),
        out_specs=pl.BlockSpec(memory_space=pltpu.VMEM),
        scratch_shapes=[
            pltpu.SemaphoreType.DMA((NR,)),
            pltpu.SemaphoreType.DMA((NR,)),
            pltpu.SemaphoreType.DMA,
        ],
        compiler_params=pltpu.CompilerParams(collective_id=0, has_side_effects=True),
        name="exchange",
    )(sent)
    start = lax.axis_index("range") * bins
    shifts = lax.dynamic_slice_in_dim(shift_table, start, bins, 0)[None]
    taps = lax.dynamic_slice_in_dim(tap_table, start, bins, 0)[None]
    own, tail = pl.pallas_call(
        migrate_kernel,
        out_shape=[jax.ShapeDtypeStruct((512, bins), BF16), jax.ShapeDtypeStruct((256, bins), BF16)],
        in_specs=vmem(4),
        out_specs=vmem(2),
        scratch_shapes=[
            pltpu.VMEM((NR * MSG, RB), F32),
            pltpu.VMEM((512, 6 * RB), BF16),
            pltpu.VMEM((2, 512, 256), BF16),
        ],
        name="migrate",
    )(got, shifts, taps, kernels.T)
    count = lax.axis_size("pulse")
    tail = lax.ppermute(tail, "pulse", [(i, i + 1) for i in range(count - 1)])
    w, u = azimuth_constants()
    lens = jnp.repeat(tail_lengths, RBLK)[None]
    return pl.pallas_call(
        azimuth_kernel,
        out_shape=jax.ShapeDtypeStruct((2, 256, bins), BF16),
        in_specs=vmem(6),
        out_specs=pl.BlockSpec(memory_space=pltpu.VMEM),
        scratch_shapes=[pltpu.VMEM((256, 256), BF16), pltpu.VMEM((768, 256), BF16)],
        name="azimuth",
    )(own, tail, lens, azimuth_rate[None], w, u)


def solution(mesh):
    in_specs = (P(None, ("pulse", "range"), None), P(), P(), P(), P(), P("range"), P("range"))
    return jax.shard_map(
        per_device, mesh=mesh, in_specs=in_specs, out_specs=P(None, "pulse", "range"), check_vma=False
    )
```

profile of v0, /device:TPU:70, one launch (start us, length us, event | category | flops | bytes accessed | tf_op | source)
XLA Modules:
  0.0 70.0 jit_solution(6071413255409157375)
XLA Ops:
  0.0 1.3 %dynamic_slice.6 = s32[512]{0:T(512)} dynamic-slice(s32[32768]{0:T(1024)} %param.16, s32[]{:T(128)S(6)} %select_n.4), dynamic_slice_sizes={512} | dynamic-slice | bytes 4100 | tf_op jit(solution)/shard_map/dynamic_slice | solution.py:276
  1.3 1.3 %dynamic_slice.7 = s32[512]{0:T(512)} dynamic-slice(s32[32768]{0:T(1024)} %param.17, s32[]{:T(128)S(6)} %select_n.4), dynamic_slice_sizes={512} | dynamic-slice | bytes 4100 | tf_op jit(solution)/shard_map/dynamic_slice | solution.py:277
  2.7 4.4 %compress.1.src_ref = bf16[64,40,128]{2,1,0:T(8,128)(2,1)} custom-call(bf16[2,1024,128]{2,1,0:T(8,128)(2,1)} %bitcast.15, f32[512,128]{1,0:T(8,128)} %bitcast.16, bf16[512,512]{1,0:T(8,128)(2,1)} %constant.24.clone.w1_ref, bf16[256,256]{1,0:T(8,128)(2,1)} %constant.25.clone.v2_ref, bf16[256,256]{1,0:T(8,128)(2,1)} %constant.26.clone.v3_ref, ...), custom_call_target="tpu_custom_call" | custom-call | tf_op jit(solution)/shard_map/compress/pallas_call | solution.py:248
  7.0 0.0 copy-start.1
  7.0 46.3 %exchange.1.x_ref = bf16[64,40,128]{2,1,0:T(8,128)(2,1)} custom-call(bf16[64,40,128]{2,1,0:T(8,128)(2,1)} %compress.1.src_ref), custom_call_target="tpu_custom_call" | custom-call | tf_op jit(solution)/shard_map/exchange/pallas_call | solution.py:262
  53.3 3.0 %migrate.1 = (bf16[512,512]{1,0:T(8,128)(2,1)}, bf16[256,512]{1,0:T(8,128)(2,1)}) custom-call(bf16[64,40,128]{2,1,0:T(8,128)(2,1)} %exchange.1.x_ref, s32[1,512]{1,0:T(1,128)} %bitcast.18, s32[1,512]{1,0:T(1,128)} %bitcast.19, f32[8,16]{1,0:T(8,128)} %bitcast.20), custom_call_target="tpu_custom_call" | custom-call | tf_op jit(solution)/shard_map/migrate/pallas_call | solution.py:278
  56.3 1.9 %collective-permute-start = (bf16[256,512]{1,0:T(8,128)(2,1)}, bf16[256,512]{1,0:T(8,128)(2,1)S(1)}, u32[]{:S(2)}, u32[]{:S(2)}) collective-permute-start(bf16[256,512]{1,0:T(8,128)(2,1)} %get-tuple-element.8), channel_id=1, source_target_pairs={{0,64},{64,128},{128,192},{192,256},{256,320},{320,384},{384,448},... | collective-permute-start | bytes 786440 | tf_op jit(solution)/shard_map/ppermute | solution.py:291
  58.2 6.0 %collective-permute-done.tail_ref = bf16[256,512]{1,0:T(8,128)(2,1)S(1)} collective-permute-done((bf16[256,512]{1,0:T(8,128)(2,1)}, bf16[256,512]{1,0:T(8,128)(2,1)S(1)}, u32[]{:S(2)}, u32[]{:S(2)}) %collective-permute-start) | collective-permute-done | bytes 262176 | tf_op jit(solution)/shard_map/ppermute | solution.py:291
  64.2 0.0 copy-start
  64.2 0.0 copy-done.1
  64.2 0.7 broadcast_in_dim.14
  64.9 0.0 copy-done
  64.9 5.1 %azimuth.1 = bf16[2,256,512]{2,1,0:T(8,128)(2,1)} custom-call(bf16[512,512]{1,0:T(8,128)(2,1)} %get-tuple-element.7.own_ref, bf16[256,512]{1,0:T(8,128)(2,1)} %copy-done, s32[1,512]{1,0:T(1,128)} %bitcast.17, f32[1,512]{1,0:T(1,128)} %bitcast.21, bf16[768,768]{1,0:T(8,128)(2,1)} %constant.29.clone.w_ref, bf16[512,768]{1,0:T(8,128)(2,1)} %constant.30.clone.u_ref), custom_call_target="tpu_custom_call" | custom-call | tf_op jit(solution)/shard_map/azimuth/pallas_call | solution.py:294
Async XLA Ops:
  7.0 57.2 %copy-start.1 = (s32[4]{0:T(128)S(1)}, s32[4]{0:T(128)}, u32[]{:S(2)}) copy-start(s32[4]{0:T(128)} %param.19) | copy-start | bytes 52
  56.3 7.9 %collective-permute-start = (bf16[256,512]{1,0:T(8,128)(2,1)}, bf16[256,512]{1,0:T(8,128)(2,1)S(1)}, u32[]{:S(2)}, u32[]{:S(2)}) collective-permute-start(bf16[256,512]{1,0:T(8,128)(2,1)} %get-tuple-element.8), channel_id=1, source_target_pairs={{0,64},{64,128},{128,192},{192,256},{256,320},{320,384},{384,448},... | collective-permute-start | bytes 786440 | tf_op jit(solution)/shard_map/ppermute | solution.py:291
  64.2 0.7 copy-start
where the time goes:
time: 70.4 us; the launch traced here: 70 us
  Pallas kernels  58.8 us (84%)
  waiting for transfers between devices  5.97 us (8%)
  local copies, waits for them, and re-layouts  3.36 us (5%)
  starting transfers between devices  1.91 us (3%)
    pallas_call x1, Pallas kernels, per_device(): pl.pallas_call(exchange_kernel, out_shape=jax.ShapeDtypeStruct((NR, MSG,...  46.3 us
    ppermute x1, waiting for transfers between devices, per_device(): tail = lax.ppermute(tail, 'pulse', [(i, i + 1) for i in range(count - 1)])  5.97 us
    pallas_call x1, Pallas kernels, per_device(): pl.pallas_call(azimuth_kernel, out_shape=jax.ShapeDtypeStruct((2, 256, bi...  5.13 us
    pallas_call x1, Pallas kernels, per_device(): pl.pallas_call(compress_kernel, out_shape=jax.ShapeDtypeStruct((NR, MSG,...  4.37 us
    pallas_call x1, Pallas kernels, per_device(): pl.pallas_call(migrate_kernel, out_shape=[jax.ShapeDtypeStruct((512, bins...  2.99 us
    ppermute x1, starting transfers between devices, per_device(): tail = lax.ppermute(tail, 'pulse', [(i, i + 1) for i in range(count - 1)])  1.91 us
  transfers between devices with their start and end apart: 1, of which 1 were waited for; matrix products, arithmetic and copies ran while one was open for 0% of the time, Pallas kernels for 0%

commit v1 on v0

v1 whole, which is shorter than its diff:
```python
import math

import jax
import jax.numpy as jnp
import numpy as np
from jax import lax
from jax.experimental import pallas as pl
from jax.experimental.pallas import tpu as pltpu
from jax.sharding import PartitionSpec as P

RA = 256
RB = 128
TMAX = 128
NK = 16
RBLK = 128
NR = 64
PD = 4
MSG = 40
F32 = jnp.float32
BF16 = jnp.bfloat16
MESH = pl.DeviceIdType.MESH


def table(rows, cols, length):
    prod = (np.asarray(rows)[:, None] * np.asarray(cols)[None, :]) % length
    angle = prod.astype(np.float32) * np.float32(-2.0 * math.pi / length)
    return np.cos(angle).astype(np.float32), np.sin(angle).astype(np.float32)


def bf(value):
    return np.asarray(value).astype(jnp.bfloat16)


def range_constants():
    ra = np.arange(RA)
    wr, wi = table(ra, ra, RA)
    vr, vi = table(np.arange(RB), np.arange(RB), RB)
    real = np.concatenate([wr, wi], 1)
    imag = np.concatenate([-wi, wr], 1)
    both = np.stack([real, imag])
    main = both.reshape(2, NR, 4, 2 * RA).transpose(1, 0, 2, 3).reshape(8 * NR, 2 * RA)
    zero = np.zeros((2, 1, 2 * RA), np.float32)
    right = np.concatenate([both[:, 4::4], zero], 1).reshape(2 * NR, 2 * RA)
    left = np.concatenate([zero, both[:, 3:-1:4]], 1).reshape(2 * NR, 2 * RA)
    inverse = bf(bf(np.concatenate([main, right, left], 0)).astype(np.float32) * np.float32(2.0**-15))
    tr, ti = table(ra, np.arange(RB), RA * RB)
    return bf(np.stack([wr, wi])), bf(np.stack([vr, vi])), inverse, np.stack([tr, ti])


def azimuth_constants():
    seq = 384
    half = seq // 2
    freq = np.concatenate([np.arange(half), [half], seq - np.arange(1, half)])
    tail = np.array([4 * s + p for p in range(PD) for s in range(NR // 2)])
    own = np.array([TMAX + 4 * s + p for p in range(PD) for s in range(NR)])
    rows = np.concatenate([own, tail])
    wr, wi = table(freq, rows, seq)
    no = own.size
    fr = [wr[:, :no], -wi[:, :no], wr[:, no:], -wi[:, no:]]
    fi = [wi[:, :no], wr[:, :no], wi[:, no:], wr[:, no:]]
    forward = bf(np.concatenate([np.concatenate(fr, 1), np.concatenate(fi, 1)], 0))
    out_rows = TMAX + np.arange(seq - TMAX)
    ur, ui = table(out_rows, freq, seq)
    inverse = bf(np.block([[ur, ui], [-ui, ur]]))
    return forward, inverse


def dot(a, b):
    return jnp.dot(a, b, preferred_element_type=F32)


def peer_order():
    def hops(offset):
        return sum(min(d, 8 - d) for d in offset)

    offsets = [(i // 8, i % 8) for i in range(1, NR)]
    return sorted(offsets, key=lambda o: -hops(o))


def sincos(phase):
    turns = phase * (2.0 / math.pi)
    near = jnp.floor(turns + 0.5)
    z = (turns - near) * (math.pi / 2)
    z2 = z * z
    sin = z * (1.0 + z2 * (-1.0 / 6 + z2 * (1.0 / 120 + z2 * (-1.0 / 5040 + z2 * (1.0 / 362880)))))
    cos = 1.0 + z2 * (-0.5 + z2 * (1.0 / 24 + z2 * (-1.0 / 720 + z2 * (1.0 / 40320))))
    quad = near.astype(jnp.int32)
    odd = (quad & 1) == 1
    s = jnp.where(odd, cos, sin)
    c = jnp.where(odd, sin, cos)
    s = jnp.where((quad & 2) == 2, -s, s)
    c = jnp.where(((quad + 1) & 2) == 2, -c, c)
    return s, c


def compress(x_ref, rf_ref, wc_ref, vc_ref, w6_ref, tw_ref, src, xs, xb, gb, hs, es, w1, v2, v3):
    for c in range(2):
        xs[c] = x_ref[c].astype(F32)
    wr, wi = wc_ref[0], wc_ref[1]
    w1[:RA, :RA] = wr
    w1[RA:, :RA] = wi
    w1[:RA, RA:] = (-wi.astype(F32)).astype(BF16)
    w1[RA:, RA:] = wr
    vr, vi = vc_ref[0], vc_ref[1]
    minus = (-vi.astype(F32)).astype(BF16)
    for ref, upper, lower in ((v2, vi, minus), (v3, minus, vi)):
        ref[:RB, :RB] = vr
        ref[:RB, RB:] = upper
        ref[RB:, :RB] = lower
        ref[RB:, RB:] = vr
    for c in range(2):
        for p in range(PD):
            xb[c * RA : (c + 1) * RA, p * RB : (p + 1) * RB] = xs[c, pl.ds(p, RA, stride=PD), :].astype(BF16)
    for c in range(2):
        for h in range(2):
            part = rf_ref[pl.ds(2 * h + c, RB, stride=4), :]
            hs[c, h * RB : (h + 1) * RB, :] = part.T
    twr, twi = tw_ref[0], tw_ref[1]
    for u in range(2):
        s1 = dot(w1[...], xb[:, 256 * u : 256 * (u + 1)])
        for v in range(2):
            p = 2 * u + v
            re = s1[:RA, v * RB : (v + 1) * RB]
            im = s1[RA:, v * RB : (v + 1) * RB]
            a = jnp.concatenate([re * twr - im * twi, re * twi + im * twr], axis=1).astype(BF16)
            t = dot(a, v2[...])
            re, im = t[:, :RB], t[:, RB:]
            hr, hi = hs[0], hs[1]
            a = jnp.concatenate([re * hr - im * hi, re * hi + im * hr], axis=1).astype(BF16)
            t = dot(a, v3[...])
            re, im = t[:, :RB], t[:, RB:]
            gb[:RA, p * RB : (p + 1) * RB] = (re * twr + im * twi).astype(BF16)
            gb[RA:, p * RB : (p + 1) * RB] = (im * twr - re * twi).astype(BF16)
    lane = lax.broadcasted_iota(jnp.int32, (2 * NR, RB), 1)
    for u in range(2):
        g = gb[:, 256 * u : 256 * (u + 1)]
        m = dot(w6_ref[: 8 * NR, :], g)
        e = dot(w6_ref[8 * NR :, :], g)
        parts = []
        for v in range(2):
            p = 2 * u + v
            parts.append(m[:, v * RB : (v + 1) * RB].reshape(NR, 8, RB))
            ev = e[:, v * RB : (v + 1) * RB]
            sel = jnp.where(lane < 64, ev[: 2 * NR], ev[2 * NR :])
            for c in range(2):
                es[pl.ds(2 * p + c, NR, stride=8), :] = sel[c * NR : (c + 1) * NR]
        src[:, 16 * u : 16 * (u + 1), :] = jnp.concatenate(parts, axis=1).astype(BF16)
    src[:, 32:40, :] = es[...].reshape(NR, 8, RB).astype(BF16)


def migration_matrix(me, shift_ref, tap_ref, kern_ref, bm):
    bm[...] = jnp.zeros_like(bm)
    for j in range(4):
        taps = tap_ref[pl.ds(4 * me + j, 1), :]
        shifts = shift_ref[pl.ds(4 * me + j, 1), :]
        coef = jnp.zeros((8, RB), F32)
        for k in range(NK):
            coef = coef + jnp.where(taps == k, kern_ref[:, k : k + 1], 0.0)
        row = lax.broadcasted_iota(jnp.int32, (160, RB), 0)
        col = lax.broadcasted_iota(jnp.int32, (160, RB), 1)
        tap = row - col - shifts - 13
        part = jnp.zeros((160, RB), F32)
        for t in range(8):
            part = part + jnp.where(tap == t, coef[t : t + 1, :], 0.0)
        top = RB * (1 + j % 2) - 16
        bm[j // 2, top : top + 160, (j % 2) * RB : (j % 2 + 1) * RB] = part.astype(BF16)


def phase_tables(rate_ref, ph, edges):
    for u in range(2):
        cols = slice(256 * u, 256 * (u + 1))
        rate = rate_ref[:, cols]
        centre = lax.broadcasted_iota(jnp.int32, (192, 256), 0).astype(F32)
        ph[0, :, cols], ph[1, :, cols] = sincos(rate * (centre * centre) * (1.0 / 384))
        edge = lax.broadcasted_iota(jnp.int32, (8, 256), 0).astype(F32)
        edge = jnp.where(edge == 0.0, 192.0, edge)
        edges[0, :, cols], edges[1, :, cols] = sincos(rate * (edge * edge) * (1.0 / 384))


def gather_blocks(got, xs, yb):
    xs[...] = got[...].reshape(NR * MSG, RB).astype(F32)
    for c in range(2):
        for p in range(PD):
            rows = slice(c * 256 + p * NR, c * 256 + (p + 1) * NR)
            halo = xs[pl.ds(32 + 2 * p + c, NR, stride=MSG), :].astype(BF16)
            yb[rows, 0:RB] = halo
            yb[rows, 5 * RB : 6 * RB] = halo
            for j in range(4):
                block = xs[pl.ds(8 * p + 4 * c + j, NR, stride=MSG), :].astype(BF16)
                yb[rows, (j + 1) * RB : (j + 2) * RB] = block


def focus_kernel(
    x_ref, rf_ref, shift_ref, tap_ref, kern_ref, len_ref, rate_ref,
    wc_ref, vc_ref, w6_ref, tw_ref, w_ref, u_ref, out_ref,
    src, got, xs, xb, gb, hs, es, w1, v2, v3, xr, yb, bm, ph, edges, mig, tsrc, tgot, zt, dd, db,
    send_sem, recv_sem, own_sem, tail_send, tail_recv,
):
    me = lax.axis_index("range")
    group = lax.axis_index("pulse")
    z, y = me // 8, lax.rem(me, 8)
    order = peer_order()
    ahead, behind = lax.rem(group + 1, 8), lax.rem(group + 7, 8)
    barrier = pltpu.get_barrier_semaphore()

    def peer_of(offset):
        return lax.rem(z + offset[0], 8) * 8 + lax.rem(y + offset[1], 8)

    for offset in order:
        pl.semaphore_signal(barrier, inc=1, device_id={"range": peer_of(offset)}, device_id_type=MESH)
    for other in (ahead, behind):
        pl.semaphore_signal(barrier, inc=1, device_id={"pulse": other}, device_id_type=MESH)
    compress(x_ref, rf_ref, wc_ref, vc_ref, w6_ref, tw_ref, src, xs, xb, gb, hs, es, w1, v2, v3)
    own = pltpu.make_async_copy(src.at[me], got.at[me], own_sem)
    own.start()
    pl.semaphore_wait(barrier, NR + 1)
    copies = []
    for i, offset in enumerate(order):
        peer = peer_of(offset)
        copy = pltpu.make_async_remote_copy(
            src_ref=src.at[peer],
            dst_ref=got.at[me],
            send_sem=send_sem.at[i],
            recv_sem=recv_sem.at[i],
            device_id={"range": peer},
            device_id_type=MESH,
        )
        copy.start()
        copies.append(copy)
    migration_matrix(me, shift_ref, tap_ref, kern_ref, bm)
    phase_tables(rate_ref, ph, edges)
    own.wait()
    for copy in copies:
        copy.wait()
    gather_blocks(got, xr, yb)
    tails = []
    for u in range(2):
        cols = slice(256 * u, 256 * (u + 1))
        part = dot(yb[:, 256 * u : 256 * u + 512], bm[u]).astype(BF16)
        mig[:, cols] = part
        for c in range(2):
            for p in range(PD):
                first = c * 256 + p * NR + 32
                tsrc[u, c * TMAX + p * 32 : c * TMAX + (p + 1) * 32, :] = part[first : first + 32]
        copy = pltpu.make_async_remote_copy(
            src_ref=tsrc.at[u],
            dst_ref=tgot.at[u],
            send_sem=tail_send.at[u],
            recv_sem=tail_recv.at[u],
            device_id={"pulse": ahead},
            device_id_type=MESH,
        )
        copy.start()
        tails.append(copy)
    for u in range(2):
        dd[u] = dot(w_ref[:, :512], mig[:, 256 * u : 256 * (u + 1)])
    row = lax.broadcasted_iota(jnp.int32, (TMAX, 256), 0)
    when = 4 * lax.rem(row, 32) + row // 32
    for u in range(2):
        cols = slice(256 * u, 256 * (u + 1))
        limit = jnp.where(group == 0, 2 * TMAX, TMAX - len_ref[:, cols])
        inside = when >= limit
        tails[u].wait()
        for c in range(2):
            part = tgot[u, c * TMAX : (c + 1) * TMAX, :].astype(F32)
            zt[c * TMAX : (c + 1) * TMAX, :] = jnp.where(inside, part, 0.0).astype(BF16)
        d = dd[u] + dot(w_ref[:, 512:], zt[...])
        for h in range(2):
            s, co = ph[0, :, cols], ph[1, :, cols]
            if h == 1:
                s = jnp.concatenate([edges[0, :, cols], s[8:]], axis=0)
                co = jnp.concatenate([edges[1, :, cols], co[8:]], axis=0)
            re = d[192 * h : 192 * (h + 1)]
            im = d[384 + 192 * h : 384 + 192 * (h + 1)]
            db[192 * h : 192 * (h + 1), :] = (re * co - im * s).astype(BF16)
            db[384 + 192 * h : 384 + 192 * (h + 1), :] = (re * s + im * co).astype(BF16)
        out = dot(u_ref[...], db[...]) * (1.0 / 384)
        out_ref[0, :, cols] = out[:256].astype(BF16)
        out_ref[1, :, cols] = out[256:].astype(BF16)


def per_device(echoes, range_filter, shift_table, tap_table, kernels, tail_lengths, azimuth_rate):
    bins = azimuth_rate.shape[0]
    x = echoes.reshape(2, PD, RA, RB).transpose(0, 2, 1, 3).reshape(2, RA * PD, RB)
    rf = range_filter.reshape(2, RA, RB).transpose(1, 0, 2).reshape(2 * RA, RB)
    wc, vc, w6, tw = range_constants()
    w, u = azimuth_constants()
    lens = jnp.repeat(tail_lengths, RBLK)[None]
    operands = (
        x, rf, shift_table.reshape(RA, RB), tap_table.reshape(RA, RB), kernels.T, lens, azimuth_rate[None],
        wc, vc, w6, tw, w, u,
    )
    return pl.pallas_call(
        focus_kernel,
        out_shape=jax.ShapeDtypeStruct((2, 256, bins), BF16),
        in_specs=[pl.BlockSpec(memory_space=pltpu.VMEM)] * len(operands),
        out_specs=pl.BlockSpec(memory_space=pltpu.VMEM),
        scratch_shapes=[
            pltpu.VMEM((NR, MSG, RB), BF16),
            pltpu.VMEM((NR, MSG, RB), BF16),
            pltpu.VMEM((2, RA * PD, RB), F32),
            pltpu.VMEM((2 * RA, PD * RB), BF16),
            pltpu.VMEM((2 * RA, PD * RB), BF16),
            pltpu.VMEM((2, RA, RB), F32),
            pltpu.VMEM((8 * NR, RB), F32),
            pltpu.VMEM((2 * RA, 2 * RA), BF16),
            pltpu.VMEM((2 * RB, 2 * RB), BF16),
            pltpu.VMEM((2 * RB, 2 * RB), BF16),
            pltpu.VMEM((NR * MSG, RB), F32),
            pltpu.VMEM((512, 6 * RB), BF16),
            pltpu.VMEM((2, 512, 256), BF16),
            pltpu.VMEM((2, 192, bins), F32),
            pltpu.VMEM((2, 8, bins), F32),
            pltpu.VMEM((512, bins), BF16),
            pltpu.VMEM((2, 2 * TMAX, 256), BF16),
            pltpu.VMEM((2, 2 * TMAX, 256), BF16),
            pltpu.VMEM((2 * TMAX, 256), BF16),
            pltpu.VMEM((2, 768, 256), F32),
            pltpu.VMEM((768, 256), BF16),
            pltpu.SemaphoreType.DMA((NR,)),
            pltpu.SemaphoreType.DMA((NR,)),
            pltpu.SemaphoreType.DMA,
            pltpu.SemaphoreType.DMA((2,)),
            pltpu.SemaphoreType.DMA((2,)),
        ],
        compiler_params=pltpu.CompilerParams(collective_id=0, has_side_effects=True),
        name="focus",
    )(*operands)


def solution(mesh):
    in_specs = (P(None, ("pulse", "range"), None), P(), P(), P(), P(), P("range"), P("range"))
    return jax.shard_map(
        per_device, mesh=mesh, in_specs=in_specs, out_specs=P(None, "pulse", "range"), check_vma=False
    )
```

time: 70.4 us -> 45.6 us (0.65)
  the two profiles are of different devices: /device:TPU:70 before, /device:TPU:64 now
where the time goes in v1:
time: 45.6 us; the launch traced here: 45.4 us
  Pallas kernels  42.2 us (93%)
  local copies, waits for them, and re-layouts  3.17 us (7%)
    pallas_call x1, Pallas kernels, per_device(): pl.pallas_call(focus_kernel, out_shape=jax.ShapeDtypeStruct((2, 256, bins...  42.2 us
    unnamed x1, local copies, waits for them, and re-layouts  1.87 us
    broadcast_in_dim x1, local copies, waits for them, and re-layouts, per_device(): lens = jnp.repeat(tail_lengths, RBLK)[None]  1.3 us

profile of v1, /device:TPU:64, one launch (start us, length us, event | category | flops | bytes accessed | tf_op | source)
XLA Modules:
  0.0 45.4 jit_solution(8134082116391118534)
XLA Ops:
  0.0 1.3 %broadcast_in_dim.6 = s32[4,128]{1,0:T(4,128)} broadcast(s32[4]{0:T(128)} %param.18), dimensions={0} | broadcast | bytes 2064 | tf_op jit(solution)/shard_map/broadcast_in_dim | solution.py:288
  1.3 42.2 %focus.1 = bf16[2,256,512]{2,1,0:T(8,128)(2,1)} custom-call(bf16[2,1024,128]{2,1,0:T(8,128)(2,1)} %bitcast.15, f32[512,128]{1,0:T(8,128)} %bitcast.16, s32[256,128]{1,0:T(8,128)} %bitcast.17, s32[256,128]{1,0:T(8,128)} %bitcast.18, f32[8,16]{1,0:T(8,128)} %bitcast.20, s32[1,512]{1,0:T(1,128)} %bitcast.19, f32[1,512]{1,0:T(1,128)} %bitcast.21, ...), custom_call_target="tpu_custom_call" | custom-call | tf_op jit(solution)/shard_map/focus/pallas_call | solution.py:293
  43.6 1.9 %copy.17 = bf16[2,256,512]{2,1,0:T(8,128)(2,1)} copy(bf16[2,256,512]{2,1,0:T(8,128)(2,1)} %focus.1) | data formatting | bytes 1048576
